TPU v7x, 32 devices: a whole 2x2x4 slice. The times are simulated.
32 devices in a mesh: row: 8 (over y, x, core), col: 4 (over z).
Axes of the slice: x: 2, y: 2, z: 4, core: 2. Of those that a mesh axis runs over, the one named last changes fastest.
Arguments:
- probes: float32 [16384, 256], P(('row', 'col')), may hold values from -6 to 6
- spectrum: float32 [32, 512], P(('row', 'col')), may hold values from 0.5 to 4
Outputs:
- leaf_basis: float32 [16384, 256], P(('row', 'col'))
- leaf_transfer: float32 [8192, 256], P(('row', 'col'))
- pair_transfer: float32 [4096, 256], P(('row', 'col'))
- group_factor: float32 [2048, 256], P(('row', 'col'))
All inputs are finite; a program needn't handle non-finite values.
Results may differ from a plain program's by a relative error of at most 0.000076.
Values sent between devices are 32-bit elements; how exact they have to be, the bound alone decides.
No kernel may reach another device: no remote copies, remote signals or barrier semaphores. Data moves between devices by JAX's collectives and lax.ppermute only.
A program may use at most 64 MiB of HBM per device.

v0:
```python
import math
import jax
import jax.numpy as jnp
from jax import lax
from jax.sharding import PartitionSpec as P


def partner(value, axis, distance):
    mask = 2**distance
    pairs = [(source, source ^ mask) for source in range(lax.axis_size(axis))]
    return lax.ppermute(value, axis, pairs)


def circle(product, length):
    angle = 2.0 * math.pi / length * (product % length).astype(jnp.float32)
    return (jnp.cos(angle), jnp.sin(angle))


def lower_solve(low, rhs):
    return jax.scipy.linalg.solve_triangular(low, rhs, lower=True)


def matmul(left, right):
    return jnp.dot(left, right, precision=lax.Precision.HIGHEST)


def local(probes, spectrum):
    rows_dev, width = probes.shape
    n_row = lax.axis_size("row")
    n_col = lax.axis_size("col")
    devices = n_row * n_col
    slab = rows_dev // devices
    total = rows_dev * devices
    col_index = lax.axis_index("col")
    flat = lax.axis_index("row") * n_col + col_index
    highest = lax.Precision.HIGHEST
    spread = lax.all_to_all(
        probes.reshape(1, rows_dev, width), ("row", "col"), split_axis=1, concat_axis=0, tiled=True
    )
    small_index = jnp.arange(devices, dtype=jnp.int32)
    cos_small, sin_small = circle(small_index[:, None] * small_index[None, :], devices)
    real_first = jnp.einsum("ka,abr->kbr", cos_small, spread, precision=highest)
    imag_first = -jnp.einsum("ka,abr->kbr", sin_small, spread, precision=highest)
    local_rows = flat * slab + jnp.arange(slab, dtype=jnp.int32)
    cos_turn, sin_turn = circle(small_index[:, None] * local_rows[None, :], total)
    cos_turn = cos_turn[:, :, None]
    sin_turn = sin_turn[:, :, None]
    turned = jnp.stack(
        [
            real_first * cos_turn + imag_first * sin_turn,
            imag_first * cos_turn - real_first * sin_turn,
        ]
    )
    columns = lax.all_to_all(turned, ("row", "col"), split_axis=1, concat_axis=2, tiled=True)
    columns = columns.reshape(2, rows_dev, width)
    big_index = jnp.arange(rows_dev, dtype=jnp.int32)
    cos_big, sin_big = circle(big_index[:, None] * big_index[None, :], rows_dev)
    real_col, imag_col = (columns[0], columns[1])
    symbol = spectrum[0][:, None]
    real_spec = (matmul(cos_big, real_col) + matmul(sin_big, imag_col)) * symbol
    imag_spec = (matmul(cos_big, imag_col) - matmul(sin_big, real_col)) * symbol
    real_back = matmul(cos_big, real_spec) - matmul(sin_big, imag_spec)
    imag_back = matmul(cos_big, imag_spec) + matmul(sin_big, real_spec)
    cos_back, sin_back = circle(big_index * flat, total)
    cos_back = cos_back[:, None]
    sin_back = sin_back[:, None]
    returned = jnp.stack(
        [real_back * cos_back - imag_back * sin_back, imag_back * cos_back + real_back * sin_back]
    )
    spectra = lax.all_to_all(
        returned.reshape(2, 1, rows_dev, width),
        ("row", "col"),
        split_axis=2,
        concat_axis=1,
        tiled=True,
    )
    partial_sample = (
        jnp.einsum("ak,kbr->abr", cos_small, spectra[0], precision=highest)
        - jnp.einsum("ak,kbr->abr", sin_small, spectra[1], precision=highest)
    ) / total
    sample = lax.all_to_all(partial_sample, ("row", "col"), split_axis=0, concat_axis=1, tiled=True)
    sample = sample.reshape(rows_dev, width)
    leaf_gram = matmul(sample.T, sample) / rows_dev
    leaf_low = jnp.linalg.cholesky(leaf_gram)
    leaf_basis = lower_solve(leaf_low, sample.T).T
    pair_gram = leaf_gram + partner(leaf_gram, "col", 0)
    group_gram = pair_gram + partner(pair_gram, "col", 1)
    pair_low = jnp.linalg.cholesky(pair_gram)
    leaf_transfer = lower_solve(pair_low, leaf_low).T
    group_low = jnp.linalg.cholesky(group_gram)
    pair_whole = lower_solve(group_low, pair_low).T
    half = width // 2
    pair_transfer = lax.dynamic_slice_in_dim(pair_whole, col_index % 2 * half, half, 0)
    quarter = width // 4
    group_factor = lax.dynamic_slice_in_dim(group_low.T, col_index % 4 * quarter, quarter, 0)
    return (leaf_basis, leaf_transfer, pair_transfer, group_factor)


def solution(mesh):
    placed = (P(("row", "col"), None), P(("row", "col"), None))
    return jax.shard_map(
        local,
        mesh=mesh,
        in_specs=placed,
        out_specs=(
            P(("row", "col"), None),
            P(("row", "col"), None),
            P(("row", "col"), None),
            P(("row", "col"), None),
        ),
        check_vma=False,
    )
```

profile of v0, /device:TPU:0, one launch (start us, length us, event | category | flops | bytes accessed | tf_op | source)
XLA Modules:
  0.0 351.0 jit_solution(7423663234639681763)
XLA Ops:
  0.6 2.2 reshape.142
  2.8 7.3 %all-to-all-start = ((f32[1,512,256]{2,0,1:T(1,128)}), f32[1,512,256]{2,0,1:T(1,128)S(1)}, u32[]{:S(2)}, u32[]{:S(2)}) async-start(f32[1,512,256]{2,0,1:T(1,128)} %reshape.142), calls=%async_computation | async-start | bytes 1048576 | tf_op jit(solution)/shard_map/all_to_all | solution.py:37
  10.3 14.2 %all-to-all-done = f32[1,512,256]{2,0,1:T(1,128)S(1)} async-done(((f32[1,512,256]{2,0,1:T(1,128)}), f32[1,512,256]{2,0,1:T(1,128)S(1)}, u32[]{:S(2)}, u32[]{:S(2)}) %all-to-all-start) | async-done | bytes 524320 | tf_op jit(solution)/shard_map/all_to_all | solution.py:37
  28.2 4.3 %all-to-all-start.1 = ((f32[2,32,16,256]{3,2,0,1:T(8,128)}), f32[2,32,16,256]{3,2,0,1:T(8,128)S(1)}, u32[]{:S(2)}, u32[]{:S(2)}) async-start(f32[2,32,16,256]{3,2,0,1:T(8,128)} %copy.54), calls=%async_computation.1 | async-start | bytes 2097152 | tf_op jit(solution)/shard_map/all_to_all | solution.py:54
  32.5 25.0 %all-to-all-done.1 = f32[2,32,16,256]{3,2,0,1:T(8,128)S(1)} async-done(((f32[2,32,16,256]{3,2,0,1:T(8,128)}), f32[2,32,16,256]{3,2,0,1:T(8,128)S(1)}, u32[]{:S(2)}, u32[]{:S(2)}) %all-to-all-start.1) | async-done | bytes 1048608 | tf_op jit(solution)/shard_map/all_to_all | solution.py:54
  57.6 5.6 %fusion.21 = f32[512,256]{1,0:T(8,128)S(1)} fusion(f32[512,256]{1,0:T(8,128)S(1)} %bitcast.154), kind=kOutput, calls=%fused_computation.45 | convolution fusion | flops 808976384 | bytes 1048576 | tf_op jit(solution)/shard_map/dot_general | solution.py:24
  63.2 5.6 %fusion.17 = f32[512,256]{1,0:T(8,128)S(1)} fusion(f32[512,256]{1,0:T(8,128)S(1)} %bitcast.156), kind=kOutput, calls=%fused_computation.43 | convolution fusion | flops 808976384 | bytes 1048576 | tf_op jit(solution)/shard_map/dot_general | solution.py:24
  68.8 5.6 %fusion = f32[512,256]{1,0:T(8,128)S(1)} fusion(f32[512,256]{1,0:T(8,128)S(1)} %fusion.21, f32[512,256]{1,0:T(8,128)S(1)} %bitcast.157, f32[512]{0:T(512)S(1)} %bitcast.158), kind=kOutput, calls=%fused_computation.13 | convolution fusion | flops 809238528 | bytes 1574912 | tf_op jit(solution)/shard_map/dot_general | solution.py:24
  74.5 5.6 %fusion.1 = f32[512,256]{1,0:T(8,128)S(1)} fusion(f32[512,256]{1,0:T(8,128)S(1)} %fusion.17, f32[512,256]{1,0:T(8,128)S(1)} %bitcast.155, f32[512]{0:T(512)S(1)} %bitcast.159), kind=kOutput, calls=%fused_computation.14 | convolution fusion | flops 809238528 | bytes 1574912 | tf_op jit(solution)/shard_map/dot_general | solution.py:24
  80.1 5.6 %fusion.15 = f32[512,256]{1,0:T(8,128)S(1)} fusion(f32[512,256]{1,0:T(8,128)S(1)} %fusion.1), kind=kOutput, calls=%fused_computation.42 | convolution fusion | flops 808976384 | bytes 1048576 | tf_op jit(solution)/shard_map/dot_general | solution.py:24
  85.7 5.6 %fusion.19 = f32[512,256]{1,0:T(8,128)S(1)} fusion(f32[512,256]{1,0:T(8,128)S(1)} %fusion), kind=kOutput, calls=%fused_computation.44 | convolution fusion | flops 808976384 | bytes 1048576 | tf_op jit(solution)/shard_map/dot_general | solution.py:24
  91.4 5.6 %convolution_add_fusion = f32[512,256]{1,0:T(8,128)S(1)} fusion(f32[512,256]{1,0:T(8,128)S(1)} %fusion.15, f32[512,256]{1,0:T(8,128)S(1)} %fusion), kind=kOutput, calls=%fused_computation.9 | convolution fusion | flops 809107456 | bytes 1572864 | tf_op jit(solution)/shard_map/dot_general | solution.py:24
  97.0 7.2 %subtract_bitcast_fusion = (f32[1,512,256]{2,1,0:T(8,128)S(1)}, f32[1,512,256]{2,1,0:T(8,128)S(1)}) fusion(f32[512,256]{1,0:T(8,128)S(1)} %convolution_add_fusion, f32[512]{0:T(512)S(1)} %get-tuple-element.108, f32[512]{0:T(512)S(1)} %get-tuple-element.109, f32[512,256]{1,0:T(8,128)S(1)} %fusion.19, f32[512,256]{1,0:T(8,128)S(1)} %fusion.1), kind=kOutput, calls=%fused_computation.37 | convolution fusion | flops 809893888 | bytes 2625536 | tf_op jit(solution)/shard_map/dot_general | solution.py:24
  105.1 29.7 %all_to_all.19 = f32[2,1,512,256]{3,0,1,2:T(2,128)S(1)} all-to-all(f32[2,1,512,256]{3,0,1,2:T(2,128)S(1)} %copy.57), channel_id=1, replica_groups=mesh['row'=8,'col'=4] {'row','col'}, dimensions={2} | all-to-all | bytes 2097152 | tf_op jit(solution)/shard_map/all_to_all | solution.py:70
  138.6 4.4 %all-to-all-start.3 = ((f32[32,16,256]{2,1,0:T(8,128)}), f32[32,16,256]{2,1,0:T(8,128)S(1)}, u32[]{:S(2)}, u32[]{:S(2)}) async-start(f32[32,16,256]{2,1,0:T(8,128)} %copy.62), calls=%async_computation.3 | async-start | bytes 1048576 | tf_op jit(solution)/shard_map/all_to_all | solution.py:81
  143.1 14.3 %all-to-all-done.3 = f32[32,16,256]{2,1,0:T(8,128)S(1)} async-done(((f32[32,16,256]{2,1,0:T(8,128)}), f32[32,16,256]{2,1,0:T(8,128)S(1)}, u32[]{:S(2)}, u32[]{:S(2)}) %all-to-all-start.3) | async-done | bytes 524320 | tf_op jit(solution)/shard_map/all_to_all | solution.py:81
  158.5 2.6 collective-permute-start
  161.3 11.7 %cholesky.172 = f32[128,128]{1,0:T(8,128)S(1)} custom-call(f32[128,128]{1,0:T(8,128)S(1)} %cholesky.270), custom_call_target="Cholesky" | custom-call | tf_op jit(solution)/shard_map/jit(cholesky)/cholesky | solution.py:84
  173.0 9.8 %custom-call.19 = f32[1,128,128]{1,2,0:T(8,128)S(1)} custom-call(f32[1,128,128]{2,1,0:T(8,128)S(1)} %get-tuple-element.101), custom_call_target="InvertDiagBlocksLowerTriangular" | custom-call | tf_op jit(solution)/shard_map/jit(cholesky)/cholesky | solution.py:84
  183.3 11.7 %cholesky.189 = f32[128,128]{1,0:T(8,128)S(1)} custom-call(f32[128,128]{1,0:T(8,128)S(1)} %convolution_subtract_fusion.6), custom_call_target="Cholesky" | custom-call | tf_op jit(solution)/shard_map/jit(cholesky)/cholesky | solution.py:84
  197.8 4.0 %while.5 = (s32[]{:T(128)}, f32[256,256]{1,0:T(8,128)S(1)}, s32[2,2]{1,0:T(2,128)S(1)}, f32[2,128,128]{2,1,0:T(8,128)S(1)}, s32[]{:T(128)}) while((s32[]{:T(128)}, f32[256,256]{1,0:T(8,128)S(1)}, s32[2,2]{1,0:T(2,128)S(1)}, f32[2,128,128]{2,1,0:T(8,128)S(1)}, s32[]{:T(128)}) %tuple.75), condition=%wide.while_cond.1, body=%wide.while_body.1.sunk | while | flops 2 | bytes 131181 | solution.py:20
  201.8 19.8 %custom-call.15 = f32[2,128,128]{1,2,0:T(8,128)S(1)} custom-call(f32[2,128,128]{2,1,0:T(8,128)S(1)} %get-tuple-element.21), custom_call_target="InvertDiagBlocksLowerTriangular" | custom-call | tf_op jit(solution)/shard_map/jit(_solve_triangular)/triangular_solve | solution.py:20
  225.3 11.7 %cholesky.206 = f32[128,128]{1,0:T(8,128)S(1)} custom-call(f32[128,128]{1,0:T(8,128)S(1)} %cholesky.273), custom_call_target="Cholesky" | custom-call | tf_op jit(solution)/shard_map/jit(cholesky)/cholesky | solution.py:88
  237.0 9.8 %custom-call.20 = f32[1,128,128]{1,2,0:T(8,128)S(1)} custom-call(f32[1,128,128]{2,1,0:T(8,128)S(1)} %get-tuple-element.97), custom_call_target="InvertDiagBlocksLowerTriangular" | custom-call | tf_op jit(solution)/shard_map/jit(cholesky)/cholesky | solution.py:88
  247.3 11.7 %cholesky.223 = f32[128,128]{1,0:T(8,128)S(1)} custom-call(f32[128,128]{1,0:T(8,128)S(1)} %slice_subtract_fusion.1), custom_call_target="Cholesky" | custom-call | tf_op jit(solution)/shard_map/jit(cholesky)/cholesky | solution.py:88
  261.7 4.0 %while.6 = (s32[]{:T(128)}, f32[256,256]{1,0:T(8,128)S(1)}, s32[2,2]{1,0:T(2,128)S(1)}, f32[2,128,128]{2,1,0:T(8,128)S(1)}, s32[]{:T(128)}) while((s32[]{:T(128)}, f32[256,256]{1,0:T(8,128)S(1)}, s32[2,2]{1,0:T(2,128)S(1)}, f32[2,128,128]{2,1,0:T(8,128)S(1)}, s32[]{:T(128)}) %tuple.84), condition=%wide.while_cond, body=%wide.while_body.sunk | while | flops 2 | bytes 131181 | solution.py:20
  265.7 19.9 %custom-call.21 = f32[2,128,128]{1,2,0:T(8,128)S(1)} custom-call(f32[2,128,128]{2,1,0:T(8,128)S(1)} %get-tuple-element.28), custom_call_target="InvertDiagBlocksLowerTriangular" | custom-call | tf_op jit(solution)/shard_map/jit(_solve_triangular)/triangular_solve | solution.py:20
  287.6 11.7 %cholesky.240 = f32[128,128]{1,0:T(8,128)S(1)} custom-call(f32[128,128]{1,0:T(8,128)S(1)} %cholesky.276), custom_call_target="Cholesky" | custom-call | tf_op jit(solution)/shard_map/jit(cholesky)/cholesky | solution.py:90
  299.4 9.8 %custom-call.22 = f32[1,128,128]{1,2,0:T(8,128)S(1)} custom-call(f32[1,128,128]{2,1,0:T(8,128)S(1)} %get-tuple-element.93), custom_call_target="InvertDiagBlocksLowerTriangular" | custom-call | tf_op jit(solution)/shard_map/jit(cholesky)/cholesky | solution.py:90
  309.9 11.7 %cholesky.257 = f32[128,128]{1,0:T(8,128)S(1)} custom-call(f32[128,128]{1,0:T(8,128)S(1)} %slice_subtract_fusion), custom_call_target="Cholesky" | custom-call | tf_op jit(solution)/shard_map/jit(cholesky)/cholesky | solution.py:90
  324.3 4.0 %while.7 = (s32[]{:T(128)}, f32[256,256]{1,0:T(8,128)S(1)}, s32[2,2]{1,0:T(2,128)S(1)}, f32[2,128,128]{2,1,0:T(8,128)S(1)}, s32[]{:T(128)}) while((s32[]{:T(128)}, f32[256,256]{1,0:T(8,128)S(1)}, s32[2,2]{1,0:T(2,128)S(1)}, f32[2,128,128]{2,1,0:T(8,128)S(1)}, s32[]{:T(128)}) %tuple.85), condition=%wide.while_cond.clone, body=%wide.while_body.clone.sunk | while | flops 2 | bytes 131181 | solution.py:20
  328.3 19.9 %custom-call.23 = f32[2,128,128]{1,2,0:T(8,128)S(1)} custom-call(f32[2,128,128]{2,1,0:T(8,128)S(1)} %get-tuple-element.29), custom_call_target="InvertDiagBlocksLowerTriangular" | custom-call | tf_op jit(solution)/shard_map/jit(_solve_triangular)/triangular_solve | solution.py:20
  (101 shorter events, 35.4 us)
Async XLA Ops:
  2.8 21.7 %all-to-all-start = ((f32[1,512,256]{2,0,1:T(1,128)}), f32[1,512,256]{2,0,1:T(1,128)S(1)}, u32[]{:S(2)}, u32[]{:S(2)}) async-start(f32[1,512,256]{2,0,1:T(1,128)} %reshape.142), calls=%async_computation | async-start | bytes 1048576 | tf_op jit(solution)/shard_map/all_to_all | solution.py:37
  28.2 29.3 %all-to-all-start.1 = ((f32[2,32,16,256]{3,2,0,1:T(8,128)}), f32[2,32,16,256]{3,2,0,1:T(8,128)S(1)}, u32[]{:S(2)}, u32[]{:S(2)}) async-start(f32[2,32,16,256]{3,2,0,1:T(8,128)} %copy.54), calls=%async_computation.1 | async-start | bytes 2097152 | tf_op jit(solution)/shard_map/all_to_all | solution.py:54
  63.2 5.6 %copy-start = (f32[1,512]{1,0:T(1,128)S(1)}, f32[1,512]{1,0:T(1,128)}, u32[]{:S(2)}) copy-start(f32[1,512]{1,0:T(1,128)} %param.6) | copy-start | bytes 6148
  138.6 18.8 %all-to-all-start.3 = ((f32[32,16,256]{2,1,0:T(8,128)}), f32[32,16,256]{2,1,0:T(8,128)S(1)}, u32[]{:S(2)}, u32[]{:S(2)}) async-start(f32[32,16,256]{2,1,0:T(8,128)} %copy.62), calls=%async_computation.3 | async-start | bytes 1048576 | tf_op jit(solution)/shard_map/all_to_all | solution.py:81
  158.5 65.7 %collective-permute-start = (f32[256,256]{0,1:T(8,128)S(1)}, f32[256,256]{0,1:T(8,128)S(1)}, u32[]{:S(2)}, u32[]{:S(2)}) collective-permute-start(f32[256,256]{0,1:T(8,128)S(1)} %fusion.3), channel_id=1, source_target_pairs={{0,1},{1,0},{2,3},{3,2},{4,5},{5,4},{6,7},{7,6},{8,9},{9,8},{10,11... | collective-permute-start | bytes 786440 | tf_op jit(solution)/shard_map/ppermute | solution.py:11
  224.2 63.2 %collective-permute-start.1 = (f32[256,256]{0,1:T(8,128)S(1)}, f32[256,256]{0,1:T(8,128)S(1)}, u32[]{:S(2)}, u32[]{:S(2)}) collective-permute-start(f32[256,256]{0,1:T(8,128)S(1)} %add.134), channel_id=1, source_target_pairs={{0,2},{1,3},{2,0},{3,1},{4,6},{5,7},{6,4},{7,5},{8,10},{9,11},{10,... | collective-permute-start | bytes 786440 | tf_op jit(solution)/shard_map/ppermute | solution.py:11
where the time goes:
time: 355 us; the launch traced here: 351 us
  other arithmetic  164 us (46%)
  matrix products  55.7 us (16%)
  waiting for transfers between devices  53.6 us (15%)
  blocking collectives  29.7 us (8%)
  local copies, waits for them, and re-layouts  22.8 us (6%)
  starting transfers between devices  19.5 us (5%)
  between operations  5.43 us (2%)
    another operation x7, other arithmetic, lower_solve(): return jax.scipy.linalg.solve_triangular(low, rhs, lower=True)  59.8 us
    dot_general x9, matrix products, matmul(): return jnp.dot(left, right, precision=lax.Precision.HIGHEST)  47.6 us
    another operation x7, other arithmetic, local(): pair_low = jnp.linalg.cholesky(pair_gram)  34.6 us
    another operation x7, other arithmetic, local(): leaf_low = jnp.linalg.cholesky(leaf_gram)  34.6 us
    another operation x7, other arithmetic, local(): group_low = jnp.linalg.cholesky(group_gram)  34.6 us
    all_to_all x1, blocking collectives, local(): lax.all_to_all(returned.reshape(2, 1, rows_dev, width), ('row', 'col'), s...  29.7 us
    all_to_all x1, waiting for transfers between devices, local(): lax.all_to_all(turned, ('row', 'col'), split_axis=1, concat_axis=2, tiled...  25 us
    all_to_all x1, waiting for transfers between devices, local(): lax.all_to_all(partial_sample, ('row', 'col'), split_axis=0, concat_axis=...  14.3 us
  transfers between devices with their start and end apart: 5, of which 3 were waited for; matrix products, arithmetic and copies ran while one was open for 35% of the time, Pallas kernels for 0%

commit v1 on v0

--- a/solution.py
+++ b/solution.py
@@ -34,8 +34,16 @@
     col_index = lax.axis_index("col")
     flat = lax.axis_index("row") * n_col + col_index
     highest = lax.Precision.HIGHEST
-    spread = lax.all_to_all(
-        probes.reshape(1, rows_dev, width), ("row", "col"), split_axis=1, concat_axis=0, tiled=True
+    spread = jnp.concatenate(
+        lax.all_to_all(
+            jnp.stack(
+                jnp.split(probes.reshape(1, rows_dev, width), lax.axis_size(("row", "col")), axis=1)
+            ),
+            ("row", "col"),
+            0,
+            0,
+        ),
+        axis=0,
     )
     small_index = jnp.arange(devices, dtype=jnp.int32)
     cos_small, sin_small = circle(small_index[:, None] * small_index[None, :], devices)

time: 355 us -> 385 us (1.085)
  local copies, waits for them, and re-layouts: 22.8 us -> 51.5 us
    unnamed x12 -> x44, local copies, waits for them, and re-layouts: 3.45 us -> 33.7 us
  transfers between devices with their start and end apart: 5 -> 5, of which waited for: 3 -> 3; matrix products, arithmetic and copies ran while one was open for 35% -> 32% of each run, Pallas kernels for 0% -> 0%
where the time goes in v1:
time: 385 us; the launch traced here: 380 us
  other arithmetic  164 us (43%)
  matrix products  55.7 us (14%)
  waiting for transfers between devices  53.6 us (14%)
  local copies, waits for them, and re-layouts  51.5 us (13%)
  blocking collectives  29.7 us (8%)
  starting transfers between devices  19.5 us (5%)
  between operations  5.46 us (1%)
    another operation x7, other arithmetic, lower_solve(): return jax.scipy.linalg.solve_triangular(low, rhs, lower=True)  59.8 us
    dot_general x9, matrix products, matmul(): return jnp.dot(left, right, precision=lax.Precision.HIGHEST)  47.6 us
    another operation x7, other arithmetic, local(): leaf_low = jnp.linalg.cholesky(leaf_gram)  34.6 us
    another operation x7, other arithmetic, local(): pair_low = jnp.linalg.cholesky(pair_gram)  34.6 us
    another operation x7, other arithmetic, local(): group_low = jnp.linalg.cholesky(group_gram)  34.6 us
    unnamed x44, local copies, waits for them, and re-layouts  33.7 us
    all_to_all x1, blocking collectives, local(): lax.all_to_all(returned.reshape(2, 1, rows_dev, width), ('row', 'col'), s...  29.7 us
    all_to_all x1, waiting for transfers between devices, local(): lax.all_to_all(turned, ('row', 'col'), split_axis=1, concat_axis=2, tiled...  25 us
  transfers between devices with their start and end apart: 5, of which 3 were waited for; matrix products, arithmetic and copies ran while one was open for 32% of the time, Pallas kernels for 0%

profile of v1, /device:TPU:0, one launch (start us, length us, event | category | flops | bytes accessed | tf_op | source)
XLA Modules:
  0.0 379.7 jit_solution(10978442054884149369)
XLA Ops:
  31.6 7.3 %all-to-all-start = ((f32[32,1,16,256]{3,2,1,0:T(8,128)}), f32[32,1,16,256]{3,2,1,0:T(8,128)S(1)}, u32[]{:S(2)}, u32[]{:S(2)}) async-start(f32[32,1,16,256]{3,2,1,0:T(8,128)} %constant_dynamic-update-slice_fusion), calls=%async_computation | async-start | bytes 1048576 | tf_op jit(solution)/shard_map/all_to_all | solution.py:38
  39.0 14.2 %all-to-all-done = f32[32,1,16,256]{3,2,1,0:T(8,128)S(1)} async-done(((f32[32,1,16,256]{3,2,1,0:T(8,128)}), f32[32,1,16,256]{3,2,1,0:T(8,128)S(1)}, u32[]{:S(2)}, u32[]{:S(2)}) %all-to-all-start) | async-done | bytes 524320 | tf_op jit(solution)/shard_map/all_to_all | solution.py:38
  55.3 1.6 copy.50
  56.9 4.3 %all-to-all-start.1 = ((f32[2,32,16,256]{3,2,0,1:T(8,128)}), f32[2,32,16,256]{3,2,0,1:T(8,128)S(1)}, u32[]{:S(2)}, u32[]{:S(2)}) async-start(f32[2,32,16,256]{3,2,0,1:T(8,128)} %copy.50), calls=%async_computation.1 | async-start | bytes 2097152 | tf_op jit(solution)/shard_map/all_to_all | solution.py:62
  61.2 25.0 %all-to-all-done.1 = f32[2,32,16,256]{3,2,0,1:T(8,128)S(1)} async-done(((f32[2,32,16,256]{3,2,0,1:T(8,128)}), f32[2,32,16,256]{3,2,0,1:T(8,128)S(1)}, u32[]{:S(2)}, u32[]{:S(2)}) %all-to-all-start.1) | async-done | bytes 1048608 | tf_op jit(solution)/shard_map/all_to_all | solution.py:62
  86.3 5.6 %fusion.24 = f32[512,256]{1,0:T(8,128)S(1)} fusion(f32[512,256]{1,0:T(8,128)S(1)} %bitcast.319), kind=kOutput, calls=%fused_computation.48 | convolution fusion | flops 808976384 | bytes 1048576 | tf_op jit(solution)/shard_map/dot_general | solution.py:24
  91.9 5.6 %fusion.20 = f32[512,256]{1,0:T(8,128)S(1)} fusion(f32[512,256]{1,0:T(8,128)S(1)} %bitcast.321), kind=kOutput, calls=%fused_computation.46 | convolution fusion | flops 808976384 | bytes 1048576 | tf_op jit(solution)/shard_map/dot_general | solution.py:24
  97.5 5.6 %fusion = f32[512,256]{1,0:T(8,128)S(1)} fusion(f32[512,256]{1,0:T(8,128)S(1)} %fusion.24, f32[512,256]{1,0:T(8,128)S(1)} %bitcast.322, f32[512]{0:T(512)S(1)} %bitcast.323), kind=kOutput, calls=%fused_computation.13 | convolution fusion | flops 809238528 | bytes 1574912 | tf_op jit(solution)/shard_map/dot_general | solution.py:24
  103.2 5.6 %fusion.1 = f32[512,256]{1,0:T(8,128)S(1)} fusion(f32[512,256]{1,0:T(8,128)S(1)} %fusion.20, f32[512,256]{1,0:T(8,128)S(1)} %bitcast.320, f32[512]{0:T(512)S(1)} %bitcast.324), kind=kOutput, calls=%fused_computation.14 | convolution fusion | flops 809238528 | bytes 1574912 | tf_op jit(solution)/shard_map/dot_general | solution.py:24
  108.8 5.6 %fusion.18 = f32[512,256]{1,0:T(8,128)S(1)} fusion(f32[512,256]{1,0:T(8,128)S(1)} %fusion.1), kind=kOutput, calls=%fused_computation.45 | convolution fusion | flops 808976384 | bytes 1048576 | tf_op jit(solution)/shard_map/dot_general | solution.py:24
  114.4 5.6 %fusion.22 = f32[512,256]{1,0:T(8,128)S(1)} fusion(f32[512,256]{1,0:T(8,128)S(1)} %fusion), kind=kOutput, calls=%fused_computation.47 | convolution fusion | flops 808976384 | bytes 1048576 | tf_op jit(solution)/shard_map/dot_general | solution.py:24
  120.1 5.6 %convolution_add_fusion = f32[512,256]{1,0:T(8,128)S(1)} fusion(f32[512,256]{1,0:T(8,128)S(1)} %fusion.18, f32[512,256]{1,0:T(8,128)S(1)} %fusion), kind=kOutput, calls=%fused_computation.9 | convolution fusion | flops 809107456 | bytes 1572864 | tf_op jit(solution)/shard_map/dot_general | solution.py:24
  125.7 7.2 %subtract_bitcast_fusion = (f32[1,512,256]{2,1,0:T(8,128)S(1)}, f32[1,512,256]{2,1,0:T(8,128)S(1)}) fusion(f32[512,256]{1,0:T(8,128)S(1)} %convolution_add_fusion, f32[512]{0:T(512)S(1)} %get-tuple-element.108, f32[512]{0:T(512)S(1)} %get-tuple-element.109, f32[512,256]{1,0:T(8,128)S(1)} %fusion.22, f32[512,256]{1,0:T(8,128)S(1)} %fusion.1), kind=kOutput, calls=%fused_computation.40 | convolution fusion | flops 809893888 | bytes 2625536 | tf_op jit(solution)/shard_map/dot_general | solution.py:24
  133.8 29.7 %all_to_all.32 = f32[2,1,512,256]{3,0,1,2:T(2,128)S(1)} all-to-all(f32[2,1,512,256]{3,0,1,2:T(2,128)S(1)} %copy.53), channel_id=1, replica_groups=mesh['row'=8,'col'=4] {'row','col'}, dimensions={2} | all-to-all | bytes 2097152 | tf_op jit(solution)/shard_map/all_to_all | solution.py:78
  167.3 4.4 %all-to-all-start.3 = ((f32[32,16,256]{2,1,0:T(8,128)}), f32[32,16,256]{2,1,0:T(8,128)S(1)}, u32[]{:S(2)}, u32[]{:S(2)}) async-start(f32[32,16,256]{2,1,0:T(8,128)} %copy.58), calls=%async_computation.3 | async-start | bytes 1048576 | tf_op jit(solution)/shard_map/all_to_all | solution.py:89
  171.8 14.3 %all-to-all-done.3 = f32[32,16,256]{2,1,0:T(8,128)S(1)} async-done(((f32[32,16,256]{2,1,0:T(8,128)}), f32[32,16,256]{2,1,0:T(8,128)S(1)}, u32[]{:S(2)}, u32[]{:S(2)}) %all-to-all-start.3) | async-done | bytes 524320 | tf_op jit(solution)/shard_map/all_to_all | solution.py:89
  187.2 2.6 collective-permute-start
  190.0 11.7 %cholesky.172 = f32[128,128]{1,0:T(8,128)S(1)} custom-call(f32[128,128]{1,0:T(8,128)S(1)} %cholesky.270), custom_call_target="Cholesky" | custom-call | tf_op jit(solution)/shard_map/jit(cholesky)/cholesky | solution.py:92
  201.7 9.8 %custom-call.19 = f32[1,128,128]{1,2,0:T(8,128)S(1)} custom-call(f32[1,128,128]{2,1,0:T(8,128)S(1)} %get-tuple-element.101), custom_call_target="InvertDiagBlocksLowerTriangular" | custom-call | tf_op jit(solution)/shard_map/jit(cholesky)/cholesky | solution.py:92
  212.0 11.7 %cholesky.189 = f32[128,128]{1,0:T(8,128)S(1)} custom-call(f32[128,128]{1,0:T(8,128)S(1)} %convolution_subtract_fusion.6), custom_call_target="Cholesky" | custom-call | tf_op jit(solution)/shard_map/jit(cholesky)/cholesky | solution.py:92
  226.5 4.0 %while.5 = (s32[]{:T(128)}, f32[256,256]{1,0:T(8,128)S(1)}, s32[2,2]{1,0:T(2,128)S(1)}, f32[2,128,128]{2,1,0:T(8,128)S(1)}, s32[]{:T(128)}) while((s32[]{:T(128)}, f32[256,256]{1,0:T(8,128)S(1)}, s32[2,2]{1,0:T(2,128)S(1)}, f32[2,128,128]{2,1,0:T(8,128)S(1)}, s32[]{:T(128)}) %tuple.75), condition=%wide.while_cond.1, body=%wide.while_body.1.sunk | while | flops 2 | bytes 131181 | solution.py:20
  230.5 19.8 %custom-call.15 = f32[2,128,128]{1,2,0:T(8,128)S(1)} custom-call(f32[2,128,128]{2,1,0:T(8,128)S(1)} %get-tuple-element.21), custom_call_target="InvertDiagBlocksLowerTriangular" | custom-call | tf_op jit(solution)/shard_map/jit(_solve_triangular)/triangular_solve | solution.py:20
  254.0 11.7 %cholesky.206 = f32[128,128]{1,0:T(8,128)S(1)} custom-call(f32[128,128]{1,0:T(8,128)S(1)} %cholesky.273), custom_call_target="Cholesky" | custom-call | tf_op jit(solution)/shard_map/jit(cholesky)/cholesky | solution.py:96
  265.7 9.8 %custom-call.20 = f32[1,128,128]{1,2,0:T(8,128)S(1)} custom-call(f32[1,128,128]{2,1,0:T(8,128)S(1)} %get-tuple-element.97), custom_call_target="InvertDiagBlocksLowerTriangular" | custom-call | tf_op jit(solution)/shard_map/jit(cholesky)/cholesky | solution.py:96
  276.0 11.7 %cholesky.223 = f32[128,128]{1,0:T(8,128)S(1)} custom-call(f32[128,128]{1,0:T(8,128)S(1)} %slice_subtract_fusion.1), custom_call_target="Cholesky" | custom-call | tf_op jit(solution)/shard_map/jit(cholesky)/cholesky | solution.py:96
  290.4 4.0 %while.6 = (s32[]{:T(128)}, f32[256,256]{1,0:T(8,128)S(1)}, s32[2,2]{1,0:T(2,128)S(1)}, f32[2,128,128]{2,1,0:T(8,128)S(1)}, s32[]{:T(128)}) while((s32[]{:T(128)}, f32[256,256]{1,0:T(8,128)S(1)}, s32[2,2]{1,0:T(2,128)S(1)}, f32[2,128,128]{2,1,0:T(8,128)S(1)}, s32[]{:T(128)}) %tuple.84), condition=%wide.while_cond, body=%wide.while_body.sunk | while | flops 2 | bytes 131181 | solution.py:20
  294.4 19.9 %custom-call.21 = f32[2,128,128]{1,2,0:T(8,128)S(1)} custom-call(f32[2,128,128]{2,1,0:T(8,128)S(1)} %get-tuple-element.28), custom_call_target="InvertDiagBlocksLowerTriangular" | custom-call | tf_op jit(solution)/shard_map/jit(_solve_triangular)/triangular_solve | solution.py:20
  316.3 11.7 %cholesky.240 = f32[128,128]{1,0:T(8,128)S(1)} custom-call(f32[128,128]{1,0:T(8,128)S(1)} %cholesky.276), custom_call_target="Cholesky" | custom-call | tf_op jit(solution)/shard_map/jit(cholesky)/cholesky | solution.py:98
  328.1 9.8 %custom-call.22 = f32[1,128,128]{1,2,0:T(8,128)S(1)} custom-call(f32[1,128,128]{2,1,0:T(8,128)S(1)} %get-tuple-element.93), custom_call_target="InvertDiagBlocksLowerTriangular" | custom-call | tf_op jit(solution)/shard_map/jit(cholesky)/cholesky | solution.py:98
  338.6 11.7 %cholesky.257 = f32[128,128]{1,0:T(8,128)S(1)} custom-call(f32[128,128]{1,0:T(8,128)S(1)} %slice_subtract_fusion), custom_call_target="Cholesky" | custom-call | tf_op jit(solution)/shard_map/jit(cholesky)/cholesky | solution.py:98
  353.0 4.0 %while.7 = (s32[]{:T(128)}, f32[256,256]{1,0:T(8,128)S(1)}, s32[2,2]{1,0:T(2,128)S(1)}, f32[2,128,128]{2,1,0:T(8,128)S(1)}, s32[]{:T(128)}) while((s32[]{:T(128)}, f32[256,256]{1,0:T(8,128)S(1)}, s32[2,2]{1,0:T(2,128)S(1)}, f32[2,128,128]{2,1,0:T(8,128)S(1)}, s32[]{:T(128)}) %tuple.85), condition=%wide.while_cond.clone, body=%wide.while_body.clone.sunk | while | flops 2 | bytes 131181 | solution.py:20
  357.0 19.9 %custom-call.23 = f32[2,128,128]{1,2,0:T(8,128)S(1)} custom-call(f32[2,128,128]{2,1,0:T(8,128)S(1)} %get-tuple-element.29), custom_call_target="InvertDiagBlocksLowerTriangular" | custom-call | tf_op jit(solution)/shard_map/jit(_solve_triangular)/triangular_solve | solution.py:20
  (133 shorter events, 64.7 us)
Async XLA Ops:
  0.6 21.2 %copy-start = (f32[512,256]{1,0:T(8,128)S(1)}, f32[512,256]{1,0:T(8,128)}, u32[]{:S(2)}) copy-start(f32[512,256]{1,0:T(8,128)} %param.5) | copy-start | bytes 1572868
  31.6 21.7 %all-to-all-start = ((f32[32,1,16,256]{3,2,1,0:T(8,128)}), f32[32,1,16,256]{3,2,1,0:T(8,128)S(1)}, u32[]{:S(2)}, u32[]{:S(2)}) async-start(f32[32,1,16,256]{3,2,1,0:T(8,128)} %constant_dynamic-update-slice_fusion), calls=%async_computation | async-start | bytes 1048576 | tf_op jit(solution)/shard_map/all_to_all | solution.py:38
  56.9 29.3 %all-to-all-start.1 = ((f32[2,32,16,256]{3,2,0,1:T(8,128)}), f32[2,32,16,256]{3,2,0,1:T(8,128)S(1)}, u32[]{:S(2)}, u32[]{:S(2)}) async-start(f32[2,32,16,256]{3,2,0,1:T(8,128)} %copy.50), calls=%async_computation.1 | async-start | bytes 2097152 | tf_op jit(solution)/shard_map/all_to_all | solution.py:62
  91.9 5.6 %copy-start.1 = (f32[1,512]{1,0:T(1,128)S(1)}, f32[1,512]{1,0:T(1,128)}, u32[]{:S(2)}) copy-start(f32[1,512]{1,0:T(1,128)} %param.6) | copy-start | bytes 6148
  167.3 18.8 %all-to-all-start.3 = ((f32[32,16,256]{2,1,0:T(8,128)}), f32[32,16,256]{2,1,0:T(8,128)S(1)}, u32[]{:S(2)}, u32[]{:S(2)}) async-start(f32[32,16,256]{2,1,0:T(8,128)} %copy.58), calls=%async_computation.3 | async-start | bytes 1048576 | tf_op jit(solution)/shard_map/all_to_all | solution.py:89
  187.2 65.7 %collective-permute-start = (f32[256,256]{0,1:T(8,128)S(1)}, f32[256,256]{0,1:T(8,128)S(1)}, u32[]{:S(2)}, u32[]{:S(2)}) collective-permute-start(f32[256,256]{0,1:T(8,128)S(1)} %fusion.3), channel_id=1, source_target_pairs={{0,1},{1,0},{2,3},{3,2},{4,5},{5,4},{6,7},{7,6},{8,9},{9,8},{10,11... | collective-permute-start | bytes 786440 | tf_op jit(solution)/shard_map/ppermute | solution.py:11
  252.9 63.2 %collective-permute-start.1 = (f32[256,256]{0,1:T(8,128)S(1)}, f32[256,256]{0,1:T(8,128)S(1)}, u32[]{:S(2)}, u32[]{:S(2)}) collective-permute-start(f32[256,256]{0,1:T(8,128)S(1)} %add.134), channel_id=1, source_target_pairs={{0,2},{1,3},{2,0},{3,1},{4,6},{5,7},{6,4},{7,5},{8,10},{9,11},{10,... | collective-permute-start | bytes 786440 | tf_op jit(solution)/shard_map/ppermute | solution.py:11
